TPU v7x, 512 devices: a whole 4x4x16 slice. The times are simulated.
512 devices in a mesh: leaf: 128 (over z, y, core), level: 4 (over x).
Axes of the slice: x: 4, y: 4, z: 16, core: 2. Of those that a mesh axis runs over, the one named last changes fastest.
Arguments:
- points_x: bfloat16 [256, 262144], P(None, ('leaf', 'level')), may hold values from -6 to 6
- leaf_basis: bfloat16 [512, 512, 256], P(('leaf', 'level')), may hold values from -0.25 to 0.25
- near_tiles: bfloat16 [512, 4, 512, 512], P(('leaf', 'level')), may hold values from -0.25 to 0.25
- near_cols: int32 [512, 4], P(('leaf', 'level')), may hold values from 0 to 11, as said below
- near_count: int32 [512], P(('leaf', 'level')), may hold values from 3 to 4, as said below
- transfer: bfloat16 [2, 256, 256], replicated, may hold values from -0.3125 to 0.3125
- coupling: bfloat16 [6, 2, 256, 256], replicated, may hold values from -0.375 to 0.375
- couple_mask: int32 [6, 128, 2], replicated, may hold values 0 or 1
Outputs:
- kernel_product: bfloat16 [256, 262144], P(None, ('leaf', 'level'))
Inputs may be any that keep to these rules, and one draw needn't show every extreme that they name: Slots 0, 1 and 2 of leaf L name L itself, L - 1 and L + 1 (near_cols 4 + L mod 4, one less, one more); slot 3 names any leaf of the previous, own or next group; some leaf's slot 3 names 0 and some names 11. The live slots of a leaf are its first near_count slots; in every draw some leaf has 3 and some has 4 live slots.
All inputs are finite; a program needn't handle non-finite values.
Results may differ from a plain program's by a relative error of at most 0.015.
Values may be sent and summed in bfloat16 or wider, within the bound.
A program may use at most 64 MiB of HBM per device.

v0:
```python
from functools import partial
import jax
import jax.numpy as jnp
from jax import lax
from jax.sharding import PartitionSpec as P


def shifted(value, axis, steps):
    count = lax.axis_size(axis)
    leading, last = (max(0, -steps), min(count, count - steps))
    return lax.ppermute(value, axis, [(source, source + steps) for source in range(leading, last)])


def with_halo(block, sides, width):
    for axis, dim in sides:
        count = lax.axis_size(axis)
        forward = [(i, i + 1) for i in range(count - 1)]
        backward = [(target, source) for source, target in forward]
        low = lax.ppermute(
            lax.slice_in_dim(block, block.shape[dim] - width, None, axis=dim), axis, forward
        )
        high = lax.ppermute(lax.slice_in_dim(block, 0, width, axis=dim), axis, backward)
        block = jnp.concatenate([low, block, high], axis=dim)
    return block


def in_one_piece(arrays, axis, dim, along):
    widths = [a.shape[along] for a in arrays]
    both = jnp.concatenate(arrays, axis=along)
    whole = lax.all_gather(both, axis, axis=dim, tiled=True)
    return tuple(jnp.split(whole, [sum(widths[:k]) for k in range(1, len(widths))], axis=along))


def swapped(block, axis, distance):
    count = lax.axis_size(axis)
    route = []
    for low in range(count):
        high = low | 1 << distance
        if high != low and high < count:
            route += [(low, high), (high, low)]
    return lax.ppermute(block, axis, route)


def pair_sum(lower_coef, upper_coef, transfer):
    summed = jnp.dot(lower_coef, transfer[0], preferred_element_type=jnp.float32)
    summed = summed + jnp.dot(upper_coef, transfer[1], preferred_element_type=jnp.float32)
    return summed.astype(jnp.bfloat16)


def down_one(fields, matrix):
    return lax.dot_general(
        fields, matrix, (((1,), (1,)), ((), ())), preferred_element_type=jnp.float32
    )


def partner(coefs, distance):
    return shifted(coefs, "leaf", distance)


def add_tile(column_x, tile_block, running):
    return running + jnp.dot(column_x, tile_block, preferred_element_type=jnp.float32)


def keep_same(running):
    return running


def per_device(
    points_x, leaf_basis, near_tiles, near_cols, near_count, transfer, coupling, couple_mask
):
    group_size = lax.axis_size("level")
    leaf_count = lax.axis_size("leaf")
    group_pos = lax.axis_index("level")
    leaf_pos = lax.axis_index("leaf")
    vectors, points = points_x.shape
    leaf_map = leaf_basis[0]
    slot_count = near_tiles.shape[1]
    levels = coupling.shape[0]
    group_bits = group_size.bit_length() - 1
    leaf_bits = leaf_count.bit_length() - 1
    active = min(levels, leaf_bits + 1)
    leaf_coef = jnp.dot(points_x, leaf_map, preferred_element_type=jnp.float32).astype(jnp.bfloat16)
    padded = with_halo(points_x, (("leaf", 1),), points)
    left_g, own_g, right_g, group_coef = (
        *in_one_piece((padded[:, :points], points_x, padded[:, 2 * points :]), "level", 1, 0),
        lax.all_gather(leaf_coef[None], "level", axis=0, tiled=True),
    )
    window_x = jnp.concatenate([left_g, own_g, right_g], axis=1)
    level_coefs = [group_coef[member] for member in range(group_size)]
    while len(level_coefs) > 1:
        level_coefs = [
            pair_sum(level_coefs[2 * pair_idx], level_coefs[2 * pair_idx + 1], transfer)
            for pair_idx in range(len(level_coefs) // 2)
        ]
    top_coef = level_coefs[0]
    vec_share = vectors // group_size
    top_coef = lax.dynamic_slice_in_dim(top_coef, group_pos * vec_share, vec_share, 0)
    coarse = [top_coef]
    for level_idx in range(1, active):
        bit_num = level_idx - 1
        current = coarse[-1]
        own_side = leaf_pos >> bit_num & 1
        is_upper = own_side == 1
        partner_coef = swapped(current, "leaf", bit_num)
        lower_coef = jnp.where(is_upper, partner_coef, current)
        upper_coef = jnp.where(is_upper, current, partner_coef)
        coarse.append(pair_sum(lower_coef, upper_coef, transfer))
    couplings = []
    for level_idx in range(active):
        stride = 1 << level_idx
        cluster = leaf_pos >> level_idx
        coupled = jnp.zeros(coarse[level_idx].shape, jnp.float32)
        for pick_idx, offset in enumerate((2, 3)):
            matrix = coupling[level_idx, pick_idx]
            ahead_coef = partner(coarse[level_idx], -offset * stride)
            behind = partner(coarse[level_idx], offset * stride)
            ahead_mask = couple_mask[level_idx, cluster, pick_idx].astype(jnp.float32)
            behind_mask = couple_mask[level_idx, jnp.maximum(cluster - offset, 0), pick_idx].astype(
                jnp.float32
            )
            coupled = coupled + ahead_mask * jnp.dot(
                ahead_coef, matrix, preferred_element_type=jnp.float32
            )
            coupled = coupled + behind_mask * down_one(behind, matrix)
        couplings.append(coupled)
    fields = couplings[active - 1].astype(jnp.bfloat16)
    for level_idx in range(active - 2, -1, -1):
        child_side = leaf_pos >> level_idx & 1
        fields = (down_one(fields, transfer[child_side]) + couplings[level_idx]).astype(
            jnp.bfloat16
        )
    fields = lax.all_gather(fields, "level", axis=0, tiled=True)
    for bit_num in range(group_bits - 1, -1, -1):
        child_side = group_pos >> bit_num & 1
        fields = down_one(fields, transfer[child_side]).astype(jnp.bfloat16)
    far_field = down_one(fields, leaf_map)
    tile_count = near_count[0]
    near_field = far_field
    for slot_idx in range(slot_count):
        column_x = lax.dynamic_slice_in_dim(window_x, near_cols[0, slot_idx] * points, points, 1)
        near_field = lax.cond(
            slot_idx < tile_count,
            partial(add_tile, column_x, near_tiles[0, slot_idx]),
            keep_same,
            near_field,
        )
    return near_field.astype(jnp.bfloat16)


def solution(mesh):
    in_specs = (
        P(None, ("leaf", "level")),
        P(("leaf", "level"), None, None),
        P(("leaf", "level"), None, None, None),
        P(("leaf", "level"), None),
        P(("leaf", "level")),
        P(),
        P(),
        P(),
    )
    out_specs = P(None, ("leaf", "level"))
    return jax.shard_map(
        per_device, mesh=mesh, in_specs=in_specs, out_specs=out_specs, check_vma=False
    )
```

profile of v0, /device:TPU:2, one launch (start us, length us, event | category | flops | bytes accessed | tf_op | source)
XLA Modules:
  0.0 276.6 jit_solution(5910400586805205190)
XLA Ops:
  6.5 2.6 collective-permute-start.29
  9.1 1.3 collective-permute-start.30
  10.4 1.2 convolution_convert_fusion
  11.6 15.7 %all-gather = bf16[1024,256]{1,0:T(8,128)(2,1)S(1)} all-gather(bf16[256,256]{1,0:T(8,128)(2,1)S(1)} %convolution_convert_fusion), channel_id=2, replica_groups=mesh['leaf'=128,'level'=4] {'level'}, dimensions={0}, use_global_device_ids=true | all-gather | bytes 655360 | tf_op jit(solution)/shard_map/all_gather | solution.py:86
  27.3 1.1 fusion.64
  29.3 1.3 collective-permute-start.27
  30.6 3.2 %collective-permute-start.26 = (bf16[64,256]{1,0:T(8,128)(2,1)S(1)}, bf16[64,256]{1,0:T(8,128)(2,1)S(1)}, u32[]{:S(2)}, u32[]{:S(2)}) collective-permute-start(bf16[64,256]{1,0:T(8,128)(2,1)S(1)} %fusion.166), channel_id=1, source_target_pairs={{0,8},{4,12},{8,16},{12,20},{16,24},{20,28},{24,32},{28,36},{32,40... | collective-permute-start | bytes 98312 | tf_op jit(solution)/shard_map/ppermute | solution.py:11
  33.8 3.1 %collective-permute-start = (bf16[64,256]{1,0:T(8,128)(2,1)S(1)}, bf16[64,256]{1,0:T(8,128)(2,1)S(1)}, u32[]{:S(2)}, u32[]{:S(2)}) collective-permute-start(bf16[64,256]{1,0:T(8,128)(2,1)S(1)} %fusion.166), channel_id=1, source_target_pairs={{0,4},{4,0},{8,12},{12,8},{16,20},{20,16},{24,28},{28,24},{32,36},... | collective-permute-start | bytes 98312 | tf_op jit(solution)/shard_map/ppermute | solution.py:41
  55.8 1.3 collective-permute-start.25
  57.5 3.9 %collective-permute-start.28 = (bf16[64,256]{1,0:T(8,128)(2,1)S(1)}, bf16[64,256]{1,0:T(8,128)(2,1)S(1)}, u32[]{:S(2)}, u32[]{:S(2)}) collective-permute-start(bf16[64,256]{1,0:T(8,128)(2,1)S(1)} %fusion.166), channel_id=1, source_target_pairs={{0,12},{4,16},{8,20},{12,24},{16,28},{20,32},{24,36},{28,40},{32,4... | collective-permute-start | bytes 98312 | tf_op jit(solution)/shard_map/ppermute | solution.py:11
  61.5 8.9 %collective-permute-start.24 = (bf16[64,256]{1,0:T(8,128)(2,1)S(1)}, bf16[64,256]{1,0:T(8,128)(2,1)S(1)}, u32[]{:S(2)}, u32[]{:S(2)}) collective-permute-start(bf16[64,256]{1,0:T(8,128)(2,1)S(1)} %fusion.44), channel_id=1, source_target_pairs={{0,24},{4,28},{8,32},{12,36},{16,40},{20,44},{24,48},{28,52},{32,5... | collective-permute-start | bytes 98312 | tf_op jit(solution)/shard_map/ppermute | solution.py:11
  70.6 1.9 collective-permute-start.1
  72.7 3.7 %collective-permute-done.1 = bf16[64,256]{1,0:T(8,128)(2,1)S(1)} collective-permute-done((bf16[64,256]{1,0:T(8,128)(2,1)S(1)}, bf16[64,256]{1,0:T(8,128)(2,1)S(1)}, u32[]{:S(2)}, u32[]{:S(2)}) %collective-permute-start.1) | collective-permute-done | bytes 32800 | tf_op jit(solution)/shard_map/ppermute | solution.py:41
  76.4 1.3 collective-permute-start.23
  78.0 1.4 collective-permute-start.22
  79.6 3.9 %collective-permute-done.23 = bf16[64,256]{1,0:T(8,128)(2,1)S(1)} collective-permute-done((bf16[64,256]{1,0:T(8,128)(2,1)S(1)}, bf16[64,256]{1,0:T(8,128)(2,1)S(1)}, u32[]{:S(2)}, u32[]{:S(2)}) %collective-permute-start.23) | collective-permute-done | bytes 32800 | tf_op jit(solution)/shard_map/ppermute | solution.py:11
  83.4 1.3 collective-permute-start.21
  84.9 6.1 %collective-permute-start.2 = (bf16[64,256]{1,0:T(8,128)(2,1)S(1)}, bf16[64,256]{1,0:T(8,128)(2,1)S(1)}, u32[]{:S(2)}, u32[]{:S(2)}) collective-permute-start(bf16[64,256]{1,0:T(8,128)(2,1)S(1)} %fusion.45), channel_id=1, source_target_pairs={{0,16},{16,0},{4,20},{20,4},{8,24},{24,8},{12,28},{28,12},{32,48},... | collective-permute-start | bytes 98312 | tf_op jit(solution)/shard_map/ppermute | solution.py:41
  91.1 1.7 collective-permute-done.2
  92.8 6.8 %collective-permute-start.20 = (bf16[64,256]{1,0:T(8,128)(2,1)S(1)}, bf16[64,256]{1,0:T(8,128)(2,1)S(1)}, u32[]{:S(2)}, u32[]{:S(2)}) collective-permute-start(bf16[64,256]{1,0:T(8,128)(2,1)S(1)} %fusion.45), channel_id=1, source_target_pairs={{0,48},{4,52},{8,56},{12,60},{16,64},{20,68},{24,72},{28,76},{32,8... | collective-permute-start | bytes 98312 | tf_op jit(solution)/shard_map/ppermute | solution.py:11
  99.8 1.4 collective-permute-done.20
  101.2 1.3 collective-permute-start.19
  102.6 10.0 %collective-permute-done.19 = bf16[64,256]{1,0:T(8,128)(2,1)S(1)} collective-permute-done((bf16[64,256]{1,0:T(8,128)(2,1)S(1)}, bf16[64,256]{1,0:T(8,128)(2,1)S(1)}, u32[]{:S(2)}, u32[]{:S(2)}) %collective-permute-start.19) | collective-permute-done | bytes 32800 | tf_op jit(solution)/shard_map/ppermute | solution.py:11
  112.7 5.8 %collective-permute-start.18 = (bf16[64,256]{1,0:T(8,128)(2,1)S(1)}, bf16[64,256]{1,0:T(8,128)(2,1)S(1)}, u32[]{:S(2)}, u32[]{:S(2)}) collective-permute-start(bf16[64,256]{1,0:T(8,128)(2,1)S(1)} %fusion.45), channel_id=1, source_target_pairs={{0,32},{4,36},{8,40},{12,44},{16,48},{20,52},{24,56},{28,60},{32,6... | collective-permute-start | bytes 98312 | tf_op jit(solution)/shard_map/ppermute | solution.py:11
  118.6 1.4 collective-permute-done.18
  120.0 1.3 collective-permute-start.17
  121.7 10.8 %collective-permute-start.16 = (bf16[64,256]{1,0:T(8,128)(2,1)S(1)}, bf16[64,256]{1,0:T(8,128)(2,1)S(1)}, u32[]{:S(2)}, u32[]{:S(2)}) collective-permute-start(bf16[64,256]{1,0:T(8,128)(2,1)S(1)} %fusion.46), channel_id=1, source_target_pairs={{0,96},{4,100},{8,104},{12,108},{16,112},{20,116},{24,120},{28,124... | collective-permute-start | bytes 98312 | tf_op jit(solution)/shard_map/ppermute | solution.py:11
  132.5 5.4 %collective-permute-start.3 = (bf16[64,256]{1,0:T(8,128)(2,1)S(1)}, bf16[64,256]{1,0:T(8,128)(2,1)S(1)}, u32[]{:S(2)}, u32[]{:S(2)}) collective-permute-start(bf16[64,256]{1,0:T(8,128)(2,1)S(1)} %fusion.46), channel_id=1, source_target_pairs={{0,32},{32,0},{4,36},{36,4},{8,40},{40,8},{12,44},{44,12},{16,48},... | collective-permute-start | bytes 98312 | tf_op jit(solution)/shard_map/ppermute | solution.py:41
  138.0 2.0 pad_maximum_fusion.1
  140.0 1.3 collective-permute-start.15
  141.6 5.2 %collective-permute-start.14 = (bf16[64,256]{1,0:T(8,128)(2,1)S(1)}, bf16[64,256]{1,0:T(8,128)(2,1)S(1)}, u32[]{:S(2)}, u32[]{:S(2)}) collective-permute-start(bf16[64,256]{1,0:T(8,128)(2,1)S(1)} %fusion.46), channel_id=1, source_target_pairs={{0,64},{4,68},{8,72},{12,76},{16,80},{20,84},{24,88},{28,92},{32,9... | collective-permute-start | bytes 98312 | tf_op jit(solution)/shard_map/ppermute | solution.py:11
  147.6 1.3 collective-permute-start.13
  149.0 7.8 %collective-permute-start.4 = (bf16[64,256]{1,0:T(8,128)(2,1)S(1)}, bf16[64,256]{1,0:T(8,128)(2,1)S(1)}, u32[]{:S(2)}, u32[]{:S(2)}) collective-permute-start(bf16[64,256]{1,0:T(8,128)(2,1)S(1)} %fusion.47), channel_id=1, source_target_pairs={{0,64},{64,0},{4,68},{68,4},{8,72},{72,8},{12,76},{76,12},{16,80},... | collective-permute-start | bytes 98312 | tf_op jit(solution)/shard_map/ppermute | solution.py:41
  157.0 2.1 collective-permute-done.4
  159.0 10.5 %collective-permute-start.12 = (bf16[64,256]{1,0:T(8,128)(2,1)S(1)}, bf16[64,256]{1,0:T(8,128)(2,1)S(1)}, u32[]{:S(2)}, u32[]{:S(2)}) collective-permute-start(bf16[64,256]{1,0:T(8,128)(2,1)S(1)} %fusion.47), channel_id=1, source_target_pairs={{0,192},{4,196},{8,200},{12,204},{16,208},{20,212},{24,216},{28,22... | collective-permute-start | bytes 98312 | tf_op jit(solution)/shard_map/ppermute | solution.py:11
  169.9 1.3 collective-permute-done.12
  171.1 1.3 collective-permute-start.11
  172.6 10.4 %collective-permute-done.11 = bf16[64,256]{1,0:T(8,128)(2,1)S(1)} collective-permute-done((bf16[64,256]{1,0:T(8,128)(2,1)S(1)}, bf16[64,256]{1,0:T(8,128)(2,1)S(1)}, u32[]{:S(2)}, u32[]{:S(2)}) %collective-permute-start.11) | collective-permute-done | bytes 32800 | tf_op jit(solution)/shard_map/ppermute | solution.py:11
  182.9 5.2 %collective-permute-start.10 = (bf16[64,256]{1,0:T(8,128)(2,1)S(1)}, bf16[64,256]{1,0:T(8,128)(2,1)S(1)}, u32[]{:S(2)}, u32[]{:S(2)}) collective-permute-start(bf16[64,256]{1,0:T(8,128)(2,1)S(1)} %fusion.47), channel_id=1, source_target_pairs={{0,128},{4,132},{8,136},{12,140},{16,144},{20,148},{24,152},{28,15... | collective-permute-start | bytes 98312 | tf_op jit(solution)/shard_map/ppermute | solution.py:11
  188.3 1.4 collective-permute-done.10
  189.7 12.0 %collective-permute-start.8 = (bf16[64,256]{1,0:T(8,128)(2,1)S(1)}, bf16[64,256]{1,0:T(8,128)(2,1)S(1)}, u32[]{:S(2)}, u32[]{:S(2)}) collective-permute-start(bf16[64,256]{1,0:T(8,128)(2,1)S(1)} %fusion.48), channel_id=1, source_target_pairs={{0,384},{4,388},{8,392},{12,396},{16,400},{20,404},{24,408},{28,41... | collective-permute-start | bytes 98312 | tf_op jit(solution)/shard_map/ppermute | solution.py:11
  201.9 1.4 collective-permute-done.8
  203.3 1.3 collective-permute-start.7
  204.7 8.3 %collective-permute-done.7 = bf16[64,256]{1,0:T(8,128)(2,1)S(1)} collective-permute-done((bf16[64,256]{1,0:T(8,128)(2,1)S(1)}, bf16[64,256]{1,0:T(8,128)(2,1)S(1)}, u32[]{:S(2)}, u32[]{:S(2)}) %collective-permute-start.7) | collective-permute-done | bytes 32800 | tf_op jit(solution)/shard_map/ppermute | solution.py:11
  213.0 1.3 collective-permute-start.6
  214.4 1.4 collective-permute-done.6
  215.9 1.3 collective-permute-start.5
  217.3 13.1 %collective-permute-done.5 = bf16[64,256]{1,0:T(8,128)(2,1)S(1)} collective-permute-done((bf16[64,256]{1,0:T(8,128)(2,1)S(1)}, bf16[64,256]{1,0:T(8,128)(2,1)S(1)}, u32[]{:S(2)}, u32[]{:S(2)}) %collective-permute-start.5) | collective-permute-done | bytes 32800 | tf_op jit(solution)/shard_map/ppermute | solution.py:11
  230.4 1.3 collective-permute-start.9
  232.7 7.6 %collective-permute-done.9 = bf16[64,256]{1,0:T(8,128)(2,1)} collective-permute-done((bf16[64,256]{1,0:T(8,128)(2,1)S(1)}, bf16[64,256]{1,0:T(8,128)(2,1)}, u32[]{:S(2)}, u32[]{:S(2)}) %collective-permute-start.9) | collective-permute-done | bytes 32800 | tf_op jit(solution)/shard_map/ppermute | solution.py:11
  241.4 1.0 fusion.57
  242.4 1.0 fusion.58
  243.5 1.0 fusion.59
  244.7 12.0 %all_gather.10 = bf16[256,256]{1,0:T(8,128)(2,1)S(1)} all-gather(bf16[64,256]{1,0:T(8,128)(2,1)S(1)} %fusion.49), channel_id=1, replica_groups=mesh['leaf'=128,'level'=4] {'level'}, dimensions={0}, use_global_device_ids=true | all-gather | bytes 163840 | tf_op jit(solution)/shard_map/all_gather | solution.py:132
  257.4 2.2 fusion.217
  259.7 1.8 pad_maximum_fusion
  262.4 1.3 conditional.7
  262.4 1.3 convolution_add_fusion.1
  263.7 1.4 conditional.8
  263.7 1.3 convolution_add_fusion.2
  265.1 1.4 conditional.9
  265.1 1.3 convolution_add_fusion.3
  266.4 2.5 conditional.11
  267.7 1.3 convolution_add_fusion
  (76 shorter events, 12.6 us)
Async XLA Ops:
  6.5 3.9 %copy-start = (bf16[1,512,256]{2,1,0:T(8,128)(2,1)S(1)}, bf16[1,512,256]{2,1,0:T(8,128)(2,1)}, u32[]{:S(2)}) copy-start(bf16[1,512,256]{2,1,0:T(8,128)(2,1)} %param.17) | copy-start | bytes 786436
  6.5 21.8 %copy-start.1 = (bf16[2,256,256]{2,1,0:T(8,128)(2,1)S(1)}, bf16[2,256,256]{2,1,0:T(8,128)(2,1)}, u32[]{:S(2)}) copy-start(bf16[2,256,256]{2,1,0:T(8,128)(2,1)} %param.21) | copy-start | bytes 786436
  6.5 250.8 %all-gather.3.cloned.1.call-start = ((), (), s32[]{:S(2)}) async-start(), calls=%async_computation | async-start | bytes 3932160 | tf_op jit(solution)/shard_map/all_gather | solution.py:30
  6.5 115.1 %collective-permute-start.29 = (bf16[256,512]{1,0:T(8,128)(2,1)}, bf16[256,512]{1,0:T(8,128)(2,1)}, u32[]{:S(2)}, u32[]{:S(2)}) collective-permute-start(bf16[256,512]{1,0:T(8,128)(2,1)} %param.16), channel_id=1, source_target_pairs={{0,4},{4,8},{8,12},{12,16},{16,20},{20,24},{24,28},{28,32},{32,36}... | collective-permute-start | bytes 786440 | tf_op jit(solution)/shard_map/ppermute | solution.py:19
  9.1 123.4 %collective-permute-start.30 = (bf16[256,512]{1,0:T(8,128)(2,1)}, bf16[256,512]{1,0:T(8,128)(2,1)}, u32[]{:S(2)}, u32[]{:S(2)}) collective-permute-start(bf16[256,512]{1,0:T(8,128)(2,1)} %param.16), channel_id=1, source_target_pairs={{4,0},{8,4},{12,8},{16,12},{20,16},{24,20},{28,24},{32,28},{36,32}... | collective-permute-start | bytes 786440 | tf_op jit(solution)/shard_map/ppermute | solution.py:22
  27.3 9.6 %copy-start.7 = (s32[1,4]{1,0:T(1,128)S(1)}, s32[1,4]{1,0:T(1,128)}, u32[]{:S(2)}) copy-start(s32[1,4]{1,0:T(1,128)} %param.19) | copy-start | bytes 52
  27.3 12.8 %copy-start.6 = (s32[6,128,2]{1,2,0:T(2,128)S(1)}, s32[6,128,2]{1,2,0:T(2,128)}, u32[]{:S(2)}) copy-start(s32[6,128,2]{1,2,0:T(2,128)} %param.23) | copy-start | bytes 18436
  28.6 32.8 %copy-start.2 = (bf16[6,2,256,256]{3,2,1,0:T(8,128)(2,1)S(1)}, bf16[6,2,256,256]{3,2,1,0:T(8,128)(2,1)}, u32[]{:S(2)}) copy-start(bf16[6,2,256,256]{3,2,1,0:T(8,128)(2,1)} %param.22) | copy-start | bytes 4718596
  29.3 28.2 %collective-permute-start.27 = (bf16[64,256]{1,0:T(8,128)(2,1)S(1)}, bf16[64,256]{1,0:T(8,128)(2,1)S(1)}, u32[]{:S(2)}, u32[]{:S(2)}) collective-permute-start(bf16[64,256]{1,0:T(8,128)(2,1)S(1)} %fusion.166), channel_id=1, source_target_pairs={{12,0},{16,4},{20,8},{24,12},{28,16},{32,20},{36,24},{40,28},{44,3... | collective-permute-start | bytes 98312 | tf_op jit(solution)/shard_map/ppermute | solution.py:11
  30.6 30.9 %collective-permute-start.26 = (bf16[64,256]{1,0:T(8,128)(2,1)S(1)}, bf16[64,256]{1,0:T(8,128)(2,1)S(1)}, u32[]{:S(2)}, u32[]{:S(2)}) collective-permute-start(bf16[64,256]{1,0:T(8,128)(2,1)S(1)} %fusion.166), channel_id=1, source_target_pairs={{0,8},{4,12},{8,16},{12,20},{16,24},{20,28},{24,32},{28,36},{32,40... | collective-permute-start | bytes 98312 | tf_op jit(solution)/shard_map/ppermute | solution.py:11
  33.8 22.0 %collective-permute-start = (bf16[64,256]{1,0:T(8,128)(2,1)S(1)}, bf16[64,256]{1,0:T(8,128)(2,1)S(1)}, u32[]{:S(2)}, u32[]{:S(2)}) collective-permute-start(bf16[64,256]{1,0:T(8,128)(2,1)S(1)} %fusion.166), channel_id=1, source_target_pairs={{0,4},{4,0},{8,12},{12,8},{16,20},{20,16},{24,28},{28,24},{32,36},... | collective-permute-start | bytes 98312 | tf_op jit(solution)/shard_map/ppermute | solution.py:41
  55.8 188.7 %collective-permute-start.25 = (bf16[64,256]{1,0:T(8,128)(2,1)S(1)}, bf16[64,256]{1,0:T(8,128)(2,1)S(1)}, u32[]{:S(2)}, u32[]{:S(2)}) collective-permute-start(bf16[64,256]{1,0:T(8,128)(2,1)S(1)} %fusion.166), channel_id=1, source_target_pairs={{8,0},{12,4},{16,8},{20,12},{24,16},{28,20},{32,24},{36,28},{40,32... | collective-permute-start | bytes 98312 | tf_op jit(solution)/shard_map/ppermute | solution.py:11
  57.5 13.2 %collective-permute-start.28 = (bf16[64,256]{1,0:T(8,128)(2,1)S(1)}, bf16[64,256]{1,0:T(8,128)(2,1)S(1)}, u32[]{:S(2)}, u32[]{:S(2)}) collective-permute-start(bf16[64,256]{1,0:T(8,128)(2,1)S(1)} %fusion.166), channel_id=1, source_target_pairs={{0,12},{4,16},{8,20},{12,24},{16,28},{20,32},{24,36},{28,40},{32,4... | collective-permute-start | bytes 98312 | tf_op jit(solution)/shard_map/ppermute | solution.py:11
  61.4 76.6 %copy-start.4 = (bf16[256,512]{1,0:T(8,128)(2,1)S(1)}, bf16[256,512]{1,0:T(8,128)(2,1)}, u32[]{:S(2)}) copy-start(bf16[256,512]{1,0:T(8,128)(2,1)} %param.16) | copy-start | bytes 786436
  61.5 16.5 %collective-permute-start.24 = (bf16[64,256]{1,0:T(8,128)(2,1)S(1)}, bf16[64,256]{1,0:T(8,128)(2,1)S(1)}, u32[]{:S(2)}, u32[]{:S(2)}) collective-permute-start(bf16[64,256]{1,0:T(8,128)(2,1)S(1)} %fusion.44), channel_id=1, source_target_pairs={{0,24},{4,28},{8,32},{12,36},{16,40},{20,44},{24,48},{28,52},{32,5... | collective-permute-start | bytes 98312 | tf_op jit(solution)/shard_map/ppermute | solution.py:11
  70.6 5.8 %collective-permute-start.1 = (bf16[64,256]{1,0:T(8,128)(2,1)S(1)}, bf16[64,256]{1,0:T(8,128)(2,1)S(1)}, u32[]{:S(2)}, u32[]{:S(2)}) collective-permute-start(bf16[64,256]{1,0:T(8,128)(2,1)S(1)} %fusion.44), channel_id=1, source_target_pairs={{0,8},{8,0},{4,12},{12,4},{16,24},{24,16},{20,28},{28,20},{32,40},... | collective-permute-start | bytes 98312 | tf_op jit(solution)/shard_map/ppermute | solution.py:41
  76.4 7.0 %collective-permute-start.23 = (bf16[64,256]{1,0:T(8,128)(2,1)S(1)}, bf16[64,256]{1,0:T(8,128)(2,1)S(1)}, u32[]{:S(2)}, u32[]{:S(2)}) collective-permute-start(bf16[64,256]{1,0:T(8,128)(2,1)S(1)} %fusion.44), channel_id=1, source_target_pairs={{24,0},{28,4},{32,8},{36,12},{40,16},{44,20},{48,24},{52,28},{56,3... | collective-permute-start | bytes 98312 | tf_op jit(solution)/shard_map/ppermute | solution.py:11
  78.0 6.8 %collective-permute-start.22 = (bf16[64,256]{1,0:T(8,128)(2,1)S(1)}, bf16[64,256]{1,0:T(8,128)(2,1)S(1)}, u32[]{:S(2)}, u32[]{:S(2)}) collective-permute-start(bf16[64,256]{1,0:T(8,128)(2,1)S(1)} %fusion.44), channel_id=1, source_target_pairs={{0,16},{4,20},{8,24},{12,28},{16,32},{20,36},{24,40},{28,44},{32,4... | collective-permute-start | bytes 98312 | tf_op jit(solution)/shard_map/ppermute | solution.py:11
  83.4 160.0 %collective-permute-start.21 = (bf16[64,256]{1,0:T(8,128)(2,1)S(1)}, bf16[64,256]{1,0:T(8,128)(2,1)}, u32[]{:S(2)}, u32[]{:S(2)}) collective-permute-start(bf16[64,256]{1,0:T(8,128)(2,1)S(1)} %fusion.44), channel_id=1, source_target_pairs={{16,0},{20,4},{24,8},{28,12},{32,16},{36,20},{40,24},{44,28},{48,3... | collective-permute-start | bytes 98312 | tf_op jit(solution)/shard_map/ppermute | solution.py:11
  84.9 7.9 %collective-permute-start.2 = (bf16[64,256]{1,0:T(8,128)(2,1)S(1)}, bf16[64,256]{1,0:T(8,128)(2,1)S(1)}, u32[]{:S(2)}, u32[]{:S(2)}) collective-permute-start(bf16[64,256]{1,0:T(8,128)(2,1)S(1)} %fusion.45), channel_id=1, source_target_pairs={{0,16},{16,0},{4,20},{20,4},{8,24},{24,8},{12,28},{28,12},{32,48},... | collective-permute-start | bytes 98312 | tf_op jit(solution)/shard_map/ppermute | solution.py:41
  92.8 8.4 %collective-permute-start.20 = (bf16[64,256]{1,0:T(8,128)(2,1)S(1)}, bf16[64,256]{1,0:T(8,128)(2,1)S(1)}, u32[]{:S(2)}, u32[]{:S(2)}) collective-permute-start(bf16[64,256]{1,0:T(8,128)(2,1)S(1)} %fusion.45), channel_id=1, source_target_pairs={{0,48},{4,52},{8,56},{12,60},{16,64},{20,68},{24,72},{28,76},{32,8... | collective-permute-start | bytes 98312 | tf_op jit(solution)/shard_map/ppermute | solution.py:11
  101.2 11.5 %collective-permute-start.19 = (bf16[64,256]{1,0:T(8,128)(2,1)S(1)}, bf16[64,256]{1,0:T(8,128)(2,1)S(1)}, u32[]{:S(2)}, u32[]{:S(2)}) collective-permute-start(bf16[64,256]{1,0:T(8,128)(2,1)S(1)} %fusion.45), channel_id=1, source_target_pairs={{48,0},{52,4},{56,8},{60,12},{64,16},{68,20},{72,24},{76,28},{80,3... | collective-permute-start | bytes 98312 | tf_op jit(solution)/shard_map/ppermute | solution.py:11
  112.7 7.4 %collective-permute-start.18 = (bf16[64,256]{1,0:T(8,128)(2,1)S(1)}, bf16[64,256]{1,0:T(8,128)(2,1)S(1)}, u32[]{:S(2)}, u32[]{:S(2)}) collective-permute-start(bf16[64,256]{1,0:T(8,128)(2,1)S(1)} %fusion.45), channel_id=1, source_target_pairs={{0,32},{4,36},{8,40},{12,44},{16,48},{20,52},{24,56},{28,60},{32,6... | collective-permute-start | bytes 98312 | tf_op jit(solution)/shard_map/ppermute | solution.py:11
  120.0 122.4 %collective-permute-start.17 = (bf16[64,256]{1,0:T(8,128)(2,1)S(1)}, bf16[64,256]{1,0:T(8,128)(2,1)}, u32[]{:S(2)}, u32[]{:S(2)}) collective-permute-start(bf16[64,256]{1,0:T(8,128)(2,1)S(1)} %fusion.45), channel_id=1, source_target_pairs={{32,0},{36,4},{40,8},{44,12},{48,16},{52,20},{56,24},{60,28},{64,3... | collective-permute-start | bytes 98312 | tf_op jit(solution)/shard_map/ppermute | solution.py:11
  121.7 19.9 %collective-permute-start.16 = (bf16[64,256]{1,0:T(8,128)(2,1)S(1)}, bf16[64,256]{1,0:T(8,128)(2,1)S(1)}, u32[]{:S(2)}, u32[]{:S(2)}) collective-permute-start(bf16[64,256]{1,0:T(8,128)(2,1)S(1)} %fusion.46), channel_id=1, source_target_pairs={{0,96},{4,100},{8,104},{12,108},{16,112},{20,116},{24,120},{28,124... | collective-permute-start | bytes 98312 | tf_op jit(solution)/shard_map/ppermute | solution.py:11
  132.5 7.5 %collective-permute-start.3 = (bf16[64,256]{1,0:T(8,128)(2,1)S(1)}, bf16[64,256]{1,0:T(8,128)(2,1)S(1)}, u32[]{:S(2)}, u32[]{:S(2)}) collective-permute-start(bf16[64,256]{1,0:T(8,128)(2,1)S(1)} %fusion.46), channel_id=1, source_target_pairs={{0,32},{32,0},{4,36},{36,4},{8,40},{40,8},{12,44},{44,12},{16,48},... | collective-permute-start | bytes 98312 | tf_op jit(solution)/shard_map/ppermute | solution.py:41
  140.0 7.6 %collective-permute-start.15 = (bf16[64,256]{1,0:T(8,128)(2,1)S(1)}, bf16[64,256]{1,0:T(8,128)(2,1)S(1)}, u32[]{:S(2)}, u32[]{:S(2)}) collective-permute-start(bf16[64,256]{1,0:T(8,128)(2,1)S(1)} %fusion.46), channel_id=1, source_target_pairs={{96,0},{100,4},{104,8},{108,12},{112,16},{116,20},{120,24},{124,28... | collective-permute-start | bytes 98312 | tf_op jit(solution)/shard_map/ppermute | solution.py:11
  141.6 7.5 %collective-permute-start.14 = (bf16[64,256]{1,0:T(8,128)(2,1)S(1)}, bf16[64,256]{1,0:T(8,128)(2,1)S(1)}, u32[]{:S(2)}, u32[]{:S(2)}) collective-permute-start(bf16[64,256]{1,0:T(8,128)(2,1)S(1)} %fusion.46), channel_id=1, source_target_pairs={{0,64},{4,68},{8,72},{12,76},{16,80},{20,84},{24,88},{28,92},{32,9... | collective-permute-start | bytes 98312 | tf_op jit(solution)/shard_map/ppermute | solution.py:11
  147.6 93.8 %collective-permute-start.13 = (bf16[64,256]{1,0:T(8,128)(2,1)S(1)}, bf16[64,256]{1,0:T(8,128)(2,1)}, u32[]{:S(2)}, u32[]{:S(2)}) collective-permute-start(bf16[64,256]{1,0:T(8,128)(2,1)S(1)} %fusion.46), channel_id=1, source_target_pairs={{64,0},{68,4},{72,8},{76,12},{80,16},{84,20},{88,24},{92,28},{96,3... | collective-permute-start | bytes 98312 | tf_op jit(solution)/shard_map/ppermute | solution.py:11
  149.0 10.0 %collective-permute-start.4 = (bf16[64,256]{1,0:T(8,128)(2,1)S(1)}, bf16[64,256]{1,0:T(8,128)(2,1)S(1)}, u32[]{:S(2)}, u32[]{:S(2)}) collective-permute-start(bf16[64,256]{1,0:T(8,128)(2,1)S(1)} %fusion.47), channel_id=1, source_target_pairs={{0,64},{64,0},{4,68},{68,4},{8,72},{72,8},{12,76},{76,12},{16,80},... | collective-permute-start | bytes 98312 | tf_op jit(solution)/shard_map/ppermute | solution.py:41
  159.0 12.1 %collective-permute-start.12 = (bf16[64,256]{1,0:T(8,128)(2,1)S(1)}, bf16[64,256]{1,0:T(8,128)(2,1)S(1)}, u32[]{:S(2)}, u32[]{:S(2)}) collective-permute-start(bf16[64,256]{1,0:T(8,128)(2,1)S(1)} %fusion.47), channel_id=1, source_target_pairs={{0,192},{4,196},{8,200},{12,204},{16,208},{20,212},{24,216},{28,22... | collective-permute-start | bytes 98312 | tf_op jit(solution)/shard_map/ppermute | solution.py:11
  171.1 11.8 %collective-permute-start.11 = (bf16[64,256]{1,0:T(8,128)(2,1)S(1)}, bf16[64,256]{1,0:T(8,128)(2,1)S(1)}, u32[]{:S(2)}, u32[]{:S(2)}) collective-permute-start(bf16[64,256]{1,0:T(8,128)(2,1)S(1)} %fusion.47), channel_id=1, source_target_pairs={{192,0},{196,4},{200,8},{204,12},{208,16},{212,20},{216,24},{220,2... | collective-permute-start | bytes 98312 | tf_op jit(solution)/shard_map/ppermute | solution.py:11
  182.9 6.8 %collective-permute-start.10 = (bf16[64,256]{1,0:T(8,128)(2,1)S(1)}, bf16[64,256]{1,0:T(8,128)(2,1)S(1)}, u32[]{:S(2)}, u32[]{:S(2)}) collective-permute-start(bf16[64,256]{1,0:T(8,128)(2,1)S(1)} %fusion.47), channel_id=1, source_target_pairs={{0,128},{4,132},{8,136},{12,140},{16,144},{20,148},{24,152},{28,15... | collective-permute-start | bytes 98312 | tf_op jit(solution)/shard_map/ppermute | solution.py:11
  189.7 13.5 %collective-permute-start.8 = (bf16[64,256]{1,0:T(8,128)(2,1)S(1)}, bf16[64,256]{1,0:T(8,128)(2,1)S(1)}, u32[]{:S(2)}, u32[]{:S(2)}) collective-permute-start(bf16[64,256]{1,0:T(8,128)(2,1)S(1)} %fusion.48), channel_id=1, source_target_pairs={{0,384},{4,388},{8,392},{12,396},{16,400},{20,404},{24,408},{28,41... | collective-permute-start | bytes 98312 | tf_op jit(solution)/shard_map/ppermute | solution.py:11
  203.3 9.7 %collective-permute-start.7 = (bf16[64,256]{1,0:T(8,128)(2,1)S(1)}, bf16[64,256]{1,0:T(8,128)(2,1)S(1)}, u32[]{:S(2)}, u32[]{:S(2)}) collective-permute-start(bf16[64,256]{1,0:T(8,128)(2,1)S(1)} %fusion.48), channel_id=1, source_target_pairs={{384,0},{388,4},{392,8},{396,12},{400,16},{404,20},{408,24},{412,2... | collective-permute-start | bytes 98312 | tf_op jit(solution)/shard_map/ppermute | solution.py:11
  213.0 2.9 %collective-permute-start.6 = (bf16[64,256]{1,0:T(8,128)(2,1)S(1)}, bf16[64,256]{1,0:T(8,128)(2,1)S(1)}, u32[]{:S(2)}, u32[]{:S(2)}) collective-permute-start(bf16[64,256]{1,0:T(8,128)(2,1)S(1)} %fusion.48), channel_id=1, source_target_pairs={{0,256},{4,260},{8,264},{12,268},{16,272},{20,276},{24,280},{28,28... | collective-permute-start | bytes 98312 | tf_op jit(solution)/shard_map/ppermute | solution.py:11
  215.9 14.5 %collective-permute-start.5 = (bf16[64,256]{1,0:T(8,128)(2,1)S(1)}, bf16[64,256]{1,0:T(8,128)(2,1)S(1)}, u32[]{:S(2)}, u32[]{:S(2)}) collective-permute-start(bf16[64,256]{1,0:T(8,128)(2,1)S(1)} %fusion.48), channel_id=1, source_target_pairs={{256,0},{260,4},{264,8},{268,12},{272,16},{276,20},{280,24},{284,2... | collective-permute-start | bytes 98312 | tf_op jit(solution)/shard_map/ppermute | solution.py:11
  230.4 1.3 copy-start.5
  230.4 10.0 %collective-permute-start.9 = (bf16[64,256]{1,0:T(8,128)(2,1)S(1)}, bf16[64,256]{1,0:T(8,128)(2,1)}, u32[]{:S(2)}, u32[]{:S(2)}) collective-permute-start(bf16[64,256]{1,0:T(8,128)(2,1)S(1)} %fusion.47), channel_id=1, source_target_pairs={{128,0},{132,4},{136,8},{140,12},{144,16},{148,20},{152,24},{156,2... | collective-permute-start | bytes 98312 | tf_op jit(solution)/shard_map/ppermute | solution.py:11
  259.6 2.7 copy-start.3
Sparse Core Ops, SparseCore 0:
  140.1 44.6 all-gather.2
where the time goes:
time: 278 us; the launch traced here: 277 us
  starting transfers between devices  118 us (42%)
  waiting for transfers between devices  69.9 us (25%)
  between operations  31.4 us (11%)
  blocking collectives  27.6 us (10%)
  matrix products  18.7 us (7%)
  local copies, waits for them, and re-layouts  5.31 us (2%)
  other arithmetic  4.5 us (2%)
    ppermute x24, starting transfers between devices, shifted(): lax.ppermute(value, axis, [(source, source + steps) for source in range(l...  90.3 us
    ppermute x24, waiting for transfers between devices, shifted(): lax.ppermute(value, axis, [(source, source + steps) for source in range(l...  62.3 us
    ppermute x5, starting transfers between devices, swapped(): return lax.ppermute(block, axis, route)  24.2 us
    all_gather x1, blocking collectives, per_device(): lax.all_gather(leaf_coef[None], 'level', axis=0, tiled=True)  15.7 us
    all_gather x1, blocking collectives, per_device(): fields = lax.all_gather(fields, 'level', axis=0, tiled=True)  12 us
    dot_general x19, matrix products, down_one(): lax.dot_general(fields, matrix, (((1,), (1,)), ((), ())), preferred_eleme...  7.76 us
    ppermute x5, waiting for transfers between devices, swapped(): return lax.ppermute(block, axis, route)  7.52 us
  transfers between devices with their start and end apart: 32, of which 16 were waited for; matrix products, arithmetic and copies ran while one was open for 6% of the time, Pallas kernels for 0%

commit v1 on v0

--- a/solution.py
+++ b/solution.py
@@ -83,7 +83,10 @@
     padded = with_halo(points_x, (("leaf", 1),), points)
     left_g, own_g, right_g, group_coef = (
         *in_one_piece((padded[:, :points], points_x, padded[:, 2 * points :]), "level", 1, 0),
-        lax.all_gather(leaf_coef[None], "level", axis=0, tiled=True),
+        jnp.concatenate(
+            lax.all_to_all(jnp.stack([leaf_coef[None]] * lax.axis_size("level")), "level", 0, 0),
+            axis=0,
+        ),
     )
     window_x = jnp.concatenate([left_g, own_g, right_g], axis=1)
     level_coefs = [group_coef[member] for member in range(group_size)]

time: 278 us -> 261 us (0.939)
  blocking collectives: 27.6 us -> 12 us
  waiting for transfers between devices: 69.9 us -> 55.9 us
  starting transfers between devices: 118 us -> 131 us
    all_gather x1 -> x0, blocking collectives: 15.7 us -> none  [per_device(): lax.all_gather(leaf_coef[None], 'level', axis=0, tiled=True)]
    ppermute x24, waiting for transfers between devices: 62.3 us -> 48.9 us  [shifted(): lax.ppermute(value, axis, [(source, source + steps) for source in range(l...]
    all_to_all x0 -> x1, starting transfers between devices: none -> 9.32 us  [per_device(): lax.all_to_all(jnp.stack([leaf_coef[None]] * lax.axis_size('level')), 'le...]
    ppermute x5, starting transfers between devices: 24.2 us -> 29.1 us  [swapped(): return lax.ppermute(block, axis, route)]
  transfers between devices with their start and end apart: 32 -> 33, of which waited for: 16 -> 13; matrix products, arithmetic and copies ran while one was open for 6% -> 5% of each run, Pallas kernels for 0% -> 0%
where the time goes in v1:
time: 261 us; the launch traced here: 260 us
  starting transfers between devices  131 us (50%)
  waiting for transfers between devices  55.9 us (21%)
  between operations  31.8 us (12%)
  matrix products  17.7 us (7%)
  blocking collectives  12 us (5%)
  local copies, waits for them, and re-layouts  7.03 us (3%)
  other arithmetic  3.48 us (1%)
    ppermute x24, starting transfers between devices, shifted(): lax.ppermute(value, axis, [(source, source + steps) for source in range(l...  90 us
    ppermute x24, waiting for transfers between devices, shifted(): lax.ppermute(value, axis, [(source, source + steps) for source in range(l...  48.9 us
    ppermute x5, starting transfers between devices, swapped(): return lax.ppermute(block, axis, route)  29.1 us
    all_gather x1, blocking collectives, per_device(): fields = lax.all_gather(fields, 'level', axis=0, tiled=True)  12 us
    all_to_all x1, starting transfers between devices, per_device(): lax.all_to_all(jnp.stack([leaf_coef[None]] * lax.axis_size('level')), 'le...  9.32 us
    dot_general x19, matrix products, down_one(): lax.dot_general(fields, matrix, (((1,), (1,)), ((), ())), preferred_eleme...  7.76 us
    ppermute x5, waiting for transfers between devices, swapped(): return lax.ppermute(block, axis, route)  6.88 us
    dot_general x4, matrix products, add_tile(): jnp.dot(column_x, tile_block, preferred_element_type=jnp.float32)  5.27 us
  transfers between devices with their start and end apart: 33, of which 13 were waited for; matrix products, arithmetic and copies ran while one was open for 5% of the time, Pallas kernels for 0%

profile of v1, /device:TPU:2, one launch (start us, length us, event | category | flops | bytes accessed | tf_op | source)
XLA Modules:
  0.0 259.6 jit_solution(4513044661727682104)
XLA Ops:
  6.5 0.9 copy-done
  7.5 1.2 convolution_convert_fusion
  9.5 9.3 %all-to-all-start = ((bf16[4,1,256,256]{3,2,1,0:T(8,128)(2,1)}), bf16[4,1,256,256]{3,2,1,0:T(8,128)(2,1)S(1)}, u32[]{:S(2)}, u32[]{:S(2)}) async-start(bf16[4,1,256,256]{3,2,1,0:T(8,128)(2,1)} %stack.3), calls=%async_computation | async-start | bytes 1048576 | tf_op jit(solution)/shard_map/all_to_all | solution.py:87
  18.8 1.3 collective-permute-start.29
  20.1 1.3 collective-permute-start.30
  41.8 3.2 %collective-permute-start = (bf16[64,256]{1,0:T(8,128)(2,1)S(1)}, bf16[64,256]{1,0:T(8,128)(2,1)S(1)}, u32[]{:S(2)}, u32[]{:S(2)}) collective-permute-start(bf16[64,256]{1,0:T(8,128)(2,1)S(1)} %fusion.160), channel_id=1, source_target_pairs={{0,4},{4,0},{8,12},{12,8},{16,20},{20,16},{24,28},{28,24},{32,36},... | collective-permute-start | bytes 98312 | tf_op jit(solution)/shard_map/ppermute | solution.py:41
  45.0 0.9 pad_maximum_fusion.1
  46.0 1.3 collective-permute-start.27
  47.3 1.3 collective-permute-start.26
  48.6 1.3 collective-permute-start.25
  49.9 7.0 %collective-permute-start.28 = (bf16[64,256]{1,0:T(8,128)(2,1)S(1)}, bf16[64,256]{1,0:T(8,128)(2,1)S(1)}, u32[]{:S(2)}, u32[]{:S(2)}) collective-permute-start(bf16[64,256]{1,0:T(8,128)(2,1)S(1)} %fusion.160), channel_id=1, source_target_pairs={{0,12},{4,16},{8,20},{12,24},{16,28},{20,32},{24,36},{28,40},{32,4... | collective-permute-start | bytes 98312 | tf_op jit(solution)/shard_map/ppermute | solution.py:11
  57.2 6.5 %collective-permute-start.24 = (bf16[64,256]{1,0:T(8,128)(2,1)S(1)}, bf16[64,256]{1,0:T(8,128)(2,1)S(1)}, u32[]{:S(2)}, u32[]{:S(2)}) collective-permute-start(bf16[64,256]{1,0:T(8,128)(2,1)S(1)} %fusion.44), channel_id=1, source_target_pairs={{0,24},{4,28},{8,32},{12,36},{16,40},{20,44},{24,48},{28,52},{32,5... | collective-permute-start | bytes 98312 | tf_op jit(solution)/shard_map/ppermute | solution.py:11
  63.7 1.3 collective-permute-start.23
  65.2 1.3 collective-permute-start.22
  66.7 7.2 %collective-permute-start.1 = (bf16[64,256]{1,0:T(8,128)(2,1)S(1)}, bf16[64,256]{1,0:T(8,128)(2,1)S(1)}, u32[]{:S(2)}, u32[]{:S(2)}) collective-permute-start(bf16[64,256]{1,0:T(8,128)(2,1)S(1)} %fusion.44), channel_id=1, source_target_pairs={{0,8},{8,0},{4,12},{12,4},{16,24},{24,16},{20,28},{28,20},{32,40},... | collective-permute-start | bytes 98312 | tf_op jit(solution)/shard_map/ppermute | solution.py:41
  74.1 1.7 collective-permute-done.1
  75.8 1.3 collective-permute-start.21
  77.4 7.4 %collective-permute-start.20 = (bf16[64,256]{1,0:T(8,128)(2,1)S(1)}, bf16[64,256]{1,0:T(8,128)(2,1)S(1)}, u32[]{:S(2)}, u32[]{:S(2)}) collective-permute-start(bf16[64,256]{1,0:T(8,128)(2,1)S(1)} %fusion.45), channel_id=1, source_target_pairs={{0,48},{4,52},{8,56},{12,60},{16,64},{20,68},{24,72},{28,76},{32,8... | collective-permute-start | bytes 98312 | tf_op jit(solution)/shard_map/ppermute | solution.py:11
  85.0 1.3 collective-permute-start.19
  86.5 5.6 %collective-permute-start.2 = (bf16[64,256]{1,0:T(8,128)(2,1)S(1)}, bf16[64,256]{1,0:T(8,128)(2,1)S(1)}, u32[]{:S(2)}, u32[]{:S(2)}) collective-permute-start(bf16[64,256]{1,0:T(8,128)(2,1)S(1)} %fusion.45), channel_id=1, source_target_pairs={{0,16},{16,0},{4,20},{20,4},{8,24},{24,8},{12,28},{28,12},{32,48},... | collective-permute-start | bytes 98312 | tf_op jit(solution)/shard_map/ppermute | solution.py:41
  92.3 1.7 collective-permute-done.2
  94.0 8.0 %collective-permute-start.18 = (bf16[64,256]{1,0:T(8,128)(2,1)S(1)}, bf16[64,256]{1,0:T(8,128)(2,1)S(1)}, u32[]{:S(2)}, u32[]{:S(2)}) collective-permute-start(bf16[64,256]{1,0:T(8,128)(2,1)S(1)} %fusion.45), channel_id=1, source_target_pairs={{0,32},{4,36},{8,40},{12,44},{16,48},{20,52},{24,56},{28,60},{32,6... | collective-permute-start | bytes 98312 | tf_op jit(solution)/shard_map/ppermute | solution.py:11
  102.3 1.3 collective-permute-start.17
  103.8 12.2 %collective-permute-start.16 = (bf16[64,256]{1,0:T(8,128)(2,1)S(1)}, bf16[64,256]{1,0:T(8,128)(2,1)S(1)}, u32[]{:S(2)}, u32[]{:S(2)}) collective-permute-start(bf16[64,256]{1,0:T(8,128)(2,1)S(1)} %fusion.46), channel_id=1, source_target_pairs={{0,96},{4,100},{8,104},{12,108},{16,112},{20,116},{24,120},{28,124... | collective-permute-start | bytes 98312 | tf_op jit(solution)/shard_map/ppermute | solution.py:11
  116.2 5.1 %collective-permute-start.3 = (bf16[64,256]{1,0:T(8,128)(2,1)S(1)}, bf16[64,256]{1,0:T(8,128)(2,1)S(1)}, u32[]{:S(2)}, u32[]{:S(2)}) collective-permute-start(bf16[64,256]{1,0:T(8,128)(2,1)S(1)} %fusion.46), channel_id=1, source_target_pairs={{0,32},{32,0},{4,36},{36,4},{8,40},{40,8},{12,44},{44,12},{16,48},... | collective-permute-start | bytes 98312 | tf_op jit(solution)/shard_map/ppermute | solution.py:41
  121.5 1.7 collective-permute-done.3
  123.2 1.3 collective-permute-start.15
  124.8 2.7 %collective-permute-start.14 = (bf16[64,256]{1,0:T(8,128)(2,1)S(1)}, bf16[64,256]{1,0:T(8,128)(2,1)S(1)}, u32[]{:S(2)}, u32[]{:S(2)}) collective-permute-start(bf16[64,256]{1,0:T(8,128)(2,1)S(1)} %fusion.46), channel_id=1, source_target_pairs={{0,64},{4,68},{8,72},{12,76},{16,80},{20,84},{24,88},{28,92},{32,9... | collective-permute-start | bytes 98312 | tf_op jit(solution)/shard_map/ppermute | solution.py:11
  127.6 3.2 %collective-permute-done.15 = bf16[64,256]{1,0:T(8,128)(2,1)S(1)} collective-permute-done((bf16[64,256]{1,0:T(8,128)(2,1)S(1)}, bf16[64,256]{1,0:T(8,128)(2,1)S(1)}, u32[]{:S(2)}, u32[]{:S(2)}) %collective-permute-start.15) | collective-permute-done | bytes 32800 | tf_op jit(solution)/shard_map/ppermute | solution.py:11
  130.8 1.3 collective-permute-start.13
  132.2 7.9 %collective-permute-start.4 = (bf16[64,256]{1,0:T(8,128)(2,1)S(1)}, bf16[64,256]{1,0:T(8,128)(2,1)S(1)}, u32[]{:S(2)}, u32[]{:S(2)}) collective-permute-start(bf16[64,256]{1,0:T(8,128)(2,1)S(1)} %fusion.47), channel_id=1, source_target_pairs={{0,64},{64,0},{4,68},{68,4},{8,72},{72,8},{12,76},{76,12},{16,80},... | collective-permute-start | bytes 98312 | tf_op jit(solution)/shard_map/ppermute | solution.py:41
  140.3 1.7 collective-permute-done.4
  142.1 9.8 %collective-permute-start.12 = (bf16[64,256]{1,0:T(8,128)(2,1)S(1)}, bf16[64,256]{1,0:T(8,128)(2,1)S(1)}, u32[]{:S(2)}, u32[]{:S(2)}) collective-permute-start(bf16[64,256]{1,0:T(8,128)(2,1)S(1)} %fusion.47), channel_id=1, source_target_pairs={{0,192},{4,196},{8,200},{12,204},{16,208},{20,212},{24,216},{28,22... | collective-permute-start | bytes 98312 | tf_op jit(solution)/shard_map/ppermute | solution.py:11
  152.2 1.3 collective-permute-done.12
  153.5 1.3 collective-permute-start.11
  154.9 10.4 %collective-permute-done.11 = bf16[64,256]{1,0:T(8,128)(2,1)S(1)} collective-permute-done((bf16[64,256]{1,0:T(8,128)(2,1)S(1)}, bf16[64,256]{1,0:T(8,128)(2,1)S(1)}, u32[]{:S(2)}, u32[]{:S(2)}) %collective-permute-start.11) | collective-permute-done | bytes 32800 | tf_op jit(solution)/shard_map/ppermute | solution.py:11
  165.3 6.3 %collective-permute-start.10 = (bf16[64,256]{1,0:T(8,128)(2,1)S(1)}, bf16[64,256]{1,0:T(8,128)(2,1)S(1)}, u32[]{:S(2)}, u32[]{:S(2)}) collective-permute-start(bf16[64,256]{1,0:T(8,128)(2,1)S(1)} %fusion.47), channel_id=1, source_target_pairs={{0,128},{4,132},{8,136},{12,140},{16,144},{20,148},{24,152},{28,15... | collective-permute-start | bytes 98312 | tf_op jit(solution)/shard_map/ppermute | solution.py:11
  171.7 1.4 collective-permute-done.10
  173.2 10.9 %collective-permute-start.8 = (bf16[64,256]{1,0:T(8,128)(2,1)S(1)}, bf16[64,256]{1,0:T(8,128)(2,1)S(1)}, u32[]{:S(2)}, u32[]{:S(2)}) collective-permute-start(bf16[64,256]{1,0:T(8,128)(2,1)S(1)} %fusion.48), channel_id=1, source_target_pairs={{0,384},{4,388},{8,392},{12,396},{16,400},{20,404},{24,408},{28,41... | collective-permute-start | bytes 98312 | tf_op jit(solution)/shard_map/ppermute | solution.py:11
  184.2 2.3 collective-permute-done.8
  186.5 1.3 collective-permute-start.7
  187.9 8.3 %collective-permute-done.7 = bf16[64,256]{1,0:T(8,128)(2,1)S(1)} collective-permute-done((bf16[64,256]{1,0:T(8,128)(2,1)S(1)}, bf16[64,256]{1,0:T(8,128)(2,1)S(1)}, u32[]{:S(2)}, u32[]{:S(2)}) %collective-permute-start.7) | collective-permute-done | bytes 32800 | tf_op jit(solution)/shard_map/ppermute | solution.py:11
  196.2 1.3 collective-permute-start.6
  197.6 1.4 collective-permute-done.6
  199.0 1.3 collective-permute-start.5
  200.5 13.1 %collective-permute-done.5 = bf16[64,256]{1,0:T(8,128)(2,1)S(1)} collective-permute-done((bf16[64,256]{1,0:T(8,128)(2,1)S(1)}, bf16[64,256]{1,0:T(8,128)(2,1)S(1)}, u32[]{:S(2)}, u32[]{:S(2)}) %collective-permute-start.5) | collective-permute-done | bytes 32800 | tf_op jit(solution)/shard_map/ppermute | solution.py:11
  213.5 1.3 collective-permute-start.9
  214.8 1.0 fusion.55
  215.9 7.5 %collective-permute-done.9 = bf16[64,256]{1,0:T(8,128)(2,1)} collective-permute-done((bf16[64,256]{1,0:T(8,128)(2,1)S(1)}, bf16[64,256]{1,0:T(8,128)(2,1)}, u32[]{:S(2)}, u32[]{:S(2)}) %collective-permute-start.9) | collective-permute-done | bytes 32800 | tf_op jit(solution)/shard_map/ppermute | solution.py:11
  223.4 1.0 fusion.56
  224.4 1.0 fusion.57
  225.5 1.0 fusion.58
  226.5 1.0 fusion.59
  227.8 12.0 %all_gather.6 = bf16[256,256]{1,0:T(8,128)(2,1)S(1)} all-gather(bf16[64,256]{1,0:T(8,128)(2,1)S(1)} %fusion.49), channel_id=1, replica_groups=mesh['leaf'=128,'level'=4] {'level'}, dimensions={0}, use_global_device_ids=true | all-gather | bytes 163840 | tf_op jit(solution)/shard_map/all_gather | solution.py:135
  240.4 2.2 fusion.211
  242.7 1.8 pad_maximum_fusion
  245.4 1.3 conditional.7
  245.4 1.3 convolution_add_fusion.1
  246.8 1.4 conditional.8
  246.8 1.3 convolution_add_fusion.2
  248.1 1.4 conditional.9
  248.1 1.3 convolution_add_fusion.3
  249.5 2.5 conditional.11
  250.7 1.3 convolution_add_fusion
  (78 shorter events, 10.9 us)
Async XLA Ops:
  6.5 1.0 copy-start
  6.5 12.3 %copy-start.4 = (bf16[256,512]{1,0:T(8,128)(2,1)S(1)}, bf16[256,512]{1,0:T(8,128)(2,1)}, u32[]{:S(2)}) copy-start(bf16[256,512]{1,0:T(8,128)(2,1)} %param.16) | copy-start | bytes 786436
  6.5 15.6 %copy-start.7 = (s32[1,4]{1,0:T(1,128)S(1)}, s32[1,4]{1,0:T(1,128)}, u32[]{:S(2)}) copy-start(s32[1,4]{1,0:T(1,128)} %param.19) | copy-start | bytes 52
  6.5 18.2 %copy-start.6 = (s32[6,128,2]{1,2,0:T(2,128)S(1)}, s32[6,128,2]{1,2,0:T(2,128)}, u32[]{:S(2)}) copy-start(s32[6,128,2]{1,2,0:T(2,128)} %param.23) | copy-start | bytes 18436
  6.5 34.2 %copy-start.1 = (bf16[2,256,256]{2,1,0:T(8,128)(2,1)S(1)}, bf16[2,256,256]{2,1,0:T(8,128)(2,1)}, u32[]{:S(2)}) copy-start(bf16[2,256,256]{2,1,0:T(8,128)(2,1)} %param.21) | copy-start | bytes 786436
  9.5 31.2 %all-to-all-start = ((bf16[4,1,256,256]{3,2,1,0:T(8,128)(2,1)}), bf16[4,1,256,256]{3,2,1,0:T(8,128)(2,1)S(1)}, u32[]{:S(2)}, u32[]{:S(2)}) async-start(bf16[4,1,256,256]{3,2,1,0:T(8,128)(2,1)} %stack.3), calls=%async_computation | async-start | bytes 1048576 | tf_op jit(solution)/shard_map/all_to_all | solution.py:87
  18.8 221.6 %all-gather.2.cloned.1.call-start = ((), (), s32[]{:S(2)}) async-start(), calls=%async_computation.1 | async-start | bytes 3932160 | tf_op jit(solution)/shard_map/all_gather | solution.py:30
  18.8 26.2 %collective-permute-start.29 = (bf16[256,512]{1,0:T(8,128)(2,1)S(1)}, bf16[256,512]{1,0:T(8,128)(2,1)S(1)}, u32[]{:S(2)}, u32[]{:S(2)}) collective-permute-start(bf16[256,512]{1,0:T(8,128)(2,1)S(1)} %copy-done.4), channel_id=1, source_target_pairs={{0,4},{4,8},{8,12},{12,16},{16,20},{20,24},{24,28},{28,32},{32,36}... | collective-permute-start | bytes 786440 | tf_op jit(solution)/shard_map/ppermute | solution.py:19
  20.1 24.9 %collective-permute-start.30 = (bf16[256,512]{1,0:T(8,128)(2,1)S(1)}, bf16[256,512]{1,0:T(8,128)(2,1)S(1)}, u32[]{:S(2)}, u32[]{:S(2)}) collective-permute-start(bf16[256,512]{1,0:T(8,128)(2,1)S(1)} %copy-done.4), channel_id=1, source_target_pairs={{4,0},{8,4},{12,8},{16,12},{20,16},{24,20},{28,24},{32,28},{36,32}... | collective-permute-start | bytes 786440 | tf_op jit(solution)/shard_map/ppermute | solution.py:22
  41.8 23.2 %copy-start.2 = (bf16[6,2,256,256]{3,2,1,0:T(8,128)(2,1)S(1)}, bf16[6,2,256,256]{3,2,1,0:T(8,128)(2,1)}, u32[]{:S(2)}) copy-start(bf16[6,2,256,256]{3,2,1,0:T(8,128)(2,1)} %param.22) | copy-start | bytes 4718596
  41.8 15.0 %collective-permute-start = (bf16[64,256]{1,0:T(8,128)(2,1)S(1)}, bf16[64,256]{1,0:T(8,128)(2,1)S(1)}, u32[]{:S(2)}, u32[]{:S(2)}) collective-permute-start(bf16[64,256]{1,0:T(8,128)(2,1)S(1)} %fusion.160), channel_id=1, source_target_pairs={{0,4},{4,0},{8,12},{12,8},{16,20},{20,16},{24,28},{28,24},{32,36},... | collective-permute-start | bytes 98312 | tf_op jit(solution)/shard_map/ppermute | solution.py:41
  46.0 17.7 %collective-permute-start.27 = (bf16[64,256]{1,0:T(8,128)(2,1)S(1)}, bf16[64,256]{1,0:T(8,128)(2,1)S(1)}, u32[]{:S(2)}, u32[]{:S(2)}) collective-permute-start(bf16[64,256]{1,0:T(8,128)(2,1)S(1)} %fusion.160), channel_id=1, source_target_pairs={{12,0},{16,4},{20,8},{24,12},{28,16},{32,20},{36,24},{40,28},{44,3... | collective-permute-start | bytes 98312 | tf_op jit(solution)/shard_map/ppermute | solution.py:11
  47.3 17.9 %collective-permute-start.26 = (bf16[64,256]{1,0:T(8,128)(2,1)S(1)}, bf16[64,256]{1,0:T(8,128)(2,1)S(1)}, u32[]{:S(2)}, u32[]{:S(2)}) collective-permute-start(bf16[64,256]{1,0:T(8,128)(2,1)S(1)} %fusion.160), channel_id=1, source_target_pairs={{0,8},{4,12},{8,16},{12,20},{16,24},{20,28},{24,32},{28,36},{32,40... | collective-permute-start | bytes 98312 | tf_op jit(solution)/shard_map/ppermute | solution.py:11
  48.6 179.0 %collective-permute-start.25 = (bf16[64,256]{1,0:T(8,128)(2,1)S(1)}, bf16[64,256]{1,0:T(8,128)(2,1)S(1)}, u32[]{:S(2)}, u32[]{:S(2)}) collective-permute-start(bf16[64,256]{1,0:T(8,128)(2,1)S(1)} %fusion.160), channel_id=1, source_target_pairs={{8,0},{12,4},{16,8},{20,12},{24,16},{28,20},{32,24},{36,28},{40,32... | collective-permute-start | bytes 98312 | tf_op jit(solution)/shard_map/ppermute | solution.py:11
  49.9 16.8 %collective-permute-start.28 = (bf16[64,256]{1,0:T(8,128)(2,1)S(1)}, bf16[64,256]{1,0:T(8,128)(2,1)S(1)}, u32[]{:S(2)}, u32[]{:S(2)}) collective-permute-start(bf16[64,256]{1,0:T(8,128)(2,1)S(1)} %fusion.160), channel_id=1, source_target_pairs={{0,12},{4,16},{8,20},{12,24},{16,28},{20,32},{24,36},{28,40},{32,4... | collective-permute-start | bytes 98312 | tf_op jit(solution)/shard_map/ppermute | solution.py:11
  57.2 20.2 %collective-permute-start.24 = (bf16[64,256]{1,0:T(8,128)(2,1)S(1)}, bf16[64,256]{1,0:T(8,128)(2,1)S(1)}, u32[]{:S(2)}, u32[]{:S(2)}) collective-permute-start(bf16[64,256]{1,0:T(8,128)(2,1)S(1)} %fusion.44), channel_id=1, source_target_pairs={{0,24},{4,28},{8,32},{12,36},{16,40},{20,44},{24,48},{28,52},{32,5... | collective-permute-start | bytes 98312 | tf_op jit(solution)/shard_map/ppermute | solution.py:11
  63.7 21.3 %collective-permute-start.23 = (bf16[64,256]{1,0:T(8,128)(2,1)S(1)}, bf16[64,256]{1,0:T(8,128)(2,1)S(1)}, u32[]{:S(2)}, u32[]{:S(2)}) collective-permute-start(bf16[64,256]{1,0:T(8,128)(2,1)S(1)} %fusion.44), channel_id=1, source_target_pairs={{24,0},{28,4},{32,8},{36,12},{40,16},{44,20},{48,24},{52,28},{56,3... | collective-permute-start | bytes 98312 | tf_op jit(solution)/shard_map/ppermute | solution.py:11
  65.2 21.3 %collective-permute-start.22 = (bf16[64,256]{1,0:T(8,128)(2,1)S(1)}, bf16[64,256]{1,0:T(8,128)(2,1)S(1)}, u32[]{:S(2)}, u32[]{:S(2)}) collective-permute-start(bf16[64,256]{1,0:T(8,128)(2,1)S(1)} %fusion.44), channel_id=1, source_target_pairs={{0,16},{4,20},{8,24},{12,28},{16,32},{20,36},{24,40},{28,44},{32,4... | collective-permute-start | bytes 98312 | tf_op jit(solution)/shard_map/ppermute | solution.py:11
  66.7 9.1 %collective-permute-start.1 = (bf16[64,256]{1,0:T(8,128)(2,1)S(1)}, bf16[64,256]{1,0:T(8,128)(2,1)S(1)}, u32[]{:S(2)}, u32[]{:S(2)}) collective-permute-start(bf16[64,256]{1,0:T(8,128)(2,1)S(1)} %fusion.44), channel_id=1, source_target_pairs={{0,8},{8,0},{4,12},{12,4},{16,24},{24,16},{20,28},{28,20},{32,40},... | collective-permute-start | bytes 98312 | tf_op jit(solution)/shard_map/ppermute | solution.py:41
  75.8 150.7 %collective-permute-start.21 = (bf16[64,256]{1,0:T(8,128)(2,1)S(1)}, bf16[64,256]{1,0:T(8,128)(2,1)}, u32[]{:S(2)}, u32[]{:S(2)}) collective-permute-start(bf16[64,256]{1,0:T(8,128)(2,1)S(1)} %fusion.44), channel_id=1, source_target_pairs={{16,0},{20,4},{24,8},{28,12},{32,16},{36,20},{40,24},{44,28},{48,3... | collective-permute-start | bytes 98312 | tf_op jit(solution)/shard_map/ppermute | solution.py:11
  77.4 24.9 %collective-permute-start.20 = (bf16[64,256]{1,0:T(8,128)(2,1)S(1)}, bf16[64,256]{1,0:T(8,128)(2,1)S(1)}, u32[]{:S(2)}, u32[]{:S(2)}) collective-permute-start(bf16[64,256]{1,0:T(8,128)(2,1)S(1)} %fusion.45), channel_id=1, source_target_pairs={{0,48},{4,52},{8,56},{12,60},{16,64},{20,68},{24,72},{28,76},{32,8... | collective-permute-start | bytes 98312 | tf_op jit(solution)/shard_map/ppermute | solution.py:11
  85.0 18.8 %collective-permute-start.19 = (bf16[64,256]{1,0:T(8,128)(2,1)S(1)}, bf16[64,256]{1,0:T(8,128)(2,1)S(1)}, u32[]{:S(2)}, u32[]{:S(2)}) collective-permute-start(bf16[64,256]{1,0:T(8,128)(2,1)S(1)} %fusion.45), channel_id=1, source_target_pairs={{48,0},{52,4},{56,8},{60,12},{64,16},{68,20},{72,24},{76,28},{80,3... | collective-permute-start | bytes 98312 | tf_op jit(solution)/shard_map/ppermute | solution.py:11
  86.5 7.5 %collective-permute-start.2 = (bf16[64,256]{1,0:T(8,128)(2,1)S(1)}, bf16[64,256]{1,0:T(8,128)(2,1)S(1)}, u32[]{:S(2)}, u32[]{:S(2)}) collective-permute-start(bf16[64,256]{1,0:T(8,128)(2,1)S(1)} %fusion.45), channel_id=1, source_target_pairs={{0,16},{16,0},{4,20},{20,4},{8,24},{24,8},{12,28},{28,12},{32,48},... | collective-permute-start | bytes 98312 | tf_op jit(solution)/shard_map/ppermute | solution.py:41
  94.0 22.2 %collective-permute-start.18 = (bf16[64,256]{1,0:T(8,128)(2,1)S(1)}, bf16[64,256]{1,0:T(8,128)(2,1)S(1)}, u32[]{:S(2)}, u32[]{:S(2)}) collective-permute-start(bf16[64,256]{1,0:T(8,128)(2,1)S(1)} %fusion.45), channel_id=1, source_target_pairs={{0,32},{4,36},{8,40},{12,44},{16,48},{20,52},{24,56},{28,60},{32,6... | collective-permute-start | bytes 98312 | tf_op jit(solution)/shard_map/ppermute | solution.py:11
  102.3 123.1 %collective-permute-start.17 = (bf16[64,256]{1,0:T(8,128)(2,1)S(1)}, bf16[64,256]{1,0:T(8,128)(2,1)}, u32[]{:S(2)}, u32[]{:S(2)}) collective-permute-start(bf16[64,256]{1,0:T(8,128)(2,1)S(1)} %fusion.45), channel_id=1, source_target_pairs={{32,0},{36,4},{40,8},{44,12},{48,16},{52,20},{56,24},{60,28},{64,3... | collective-permute-start | bytes 98312 | tf_op jit(solution)/shard_map/ppermute | solution.py:11
  103.8 21.0 %collective-permute-start.16 = (bf16[64,256]{1,0:T(8,128)(2,1)S(1)}, bf16[64,256]{1,0:T(8,128)(2,1)S(1)}, u32[]{:S(2)}, u32[]{:S(2)}) collective-permute-start(bf16[64,256]{1,0:T(8,128)(2,1)S(1)} %fusion.46), channel_id=1, source_target_pairs={{0,96},{4,100},{8,104},{12,108},{16,112},{20,116},{24,120},{28,124... | collective-permute-start | bytes 98312 | tf_op jit(solution)/shard_map/ppermute | solution.py:11
  116.2 7.0 %collective-permute-start.3 = (bf16[64,256]{1,0:T(8,128)(2,1)S(1)}, bf16[64,256]{1,0:T(8,128)(2,1)S(1)}, u32[]{:S(2)}, u32[]{:S(2)}) collective-permute-start(bf16[64,256]{1,0:T(8,128)(2,1)S(1)} %fusion.46), channel_id=1, source_target_pairs={{0,32},{32,0},{4,36},{36,4},{8,40},{40,8},{12,44},{44,12},{16,48},... | collective-permute-start | bytes 98312 | tf_op jit(solution)/shard_map/ppermute | solution.py:41
  123.2 7.6 %collective-permute-start.15 = (bf16[64,256]{1,0:T(8,128)(2,1)S(1)}, bf16[64,256]{1,0:T(8,128)(2,1)S(1)}, u32[]{:S(2)}, u32[]{:S(2)}) collective-permute-start(bf16[64,256]{1,0:T(8,128)(2,1)S(1)} %fusion.46), channel_id=1, source_target_pairs={{96,0},{100,4},{104,8},{108,12},{112,16},{116,20},{120,24},{124,28... | collective-permute-start | bytes 98312 | tf_op jit(solution)/shard_map/ppermute | solution.py:11
  124.8 7.4 %collective-permute-start.14 = (bf16[64,256]{1,0:T(8,128)(2,1)S(1)}, bf16[64,256]{1,0:T(8,128)(2,1)S(1)}, u32[]{:S(2)}, u32[]{:S(2)}) collective-permute-start(bf16[64,256]{1,0:T(8,128)(2,1)S(1)} %fusion.46), channel_id=1, source_target_pairs={{0,64},{4,68},{8,72},{12,76},{16,80},{20,84},{24,88},{28,92},{32,9... | collective-permute-start | bytes 98312 | tf_op jit(solution)/shard_map/ppermute | solution.py:11
  130.8 93.6 %collective-permute-start.13 = (bf16[64,256]{1,0:T(8,128)(2,1)S(1)}, bf16[64,256]{1,0:T(8,128)(2,1)}, u32[]{:S(2)}, u32[]{:S(2)}) collective-permute-start(bf16[64,256]{1,0:T(8,128)(2,1)S(1)} %fusion.46), channel_id=1, source_target_pairs={{64,0},{68,4},{72,8},{76,12},{80,16},{84,20},{88,24},{92,28},{96,3... | collective-permute-start | bytes 98312 | tf_op jit(solution)/shard_map/ppermute | solution.py:11
  132.2 9.8 %collective-permute-start.4 = (bf16[64,256]{1,0:T(8,128)(2,1)S(1)}, bf16[64,256]{1,0:T(8,128)(2,1)S(1)}, u32[]{:S(2)}, u32[]{:S(2)}) collective-permute-start(bf16[64,256]{1,0:T(8,128)(2,1)S(1)} %fusion.47), channel_id=1, source_target_pairs={{0,64},{64,0},{4,68},{68,4},{8,72},{72,8},{12,76},{76,12},{16,80},... | collective-permute-start | bytes 98312 | tf_op jit(solution)/shard_map/ppermute | solution.py:41
  142.1 11.4 %collective-permute-start.12 = (bf16[64,256]{1,0:T(8,128)(2,1)S(1)}, bf16[64,256]{1,0:T(8,128)(2,1)S(1)}, u32[]{:S(2)}, u32[]{:S(2)}) collective-permute-start(bf16[64,256]{1,0:T(8,128)(2,1)S(1)} %fusion.47), channel_id=1, source_target_pairs={{0,192},{4,196},{8,200},{12,204},{16,208},{20,212},{24,216},{28,22... | collective-permute-start | bytes 98312 | tf_op jit(solution)/shard_map/ppermute | solution.py:11
  153.5 11.8 %collective-permute-start.11 = (bf16[64,256]{1,0:T(8,128)(2,1)S(1)}, bf16[64,256]{1,0:T(8,128)(2,1)S(1)}, u32[]{:S(2)}, u32[]{:S(2)}) collective-permute-start(bf16[64,256]{1,0:T(8,128)(2,1)S(1)} %fusion.47), channel_id=1, source_target_pairs={{192,0},{196,4},{200,8},{204,12},{208,16},{212,20},{216,24},{220,2... | collective-permute-start | bytes 98312 | tf_op jit(solution)/shard_map/ppermute | solution.py:11
  165.3 7.8 %collective-permute-start.10 = (bf16[64,256]{1,0:T(8,128)(2,1)S(1)}, bf16[64,256]{1,0:T(8,128)(2,1)S(1)}, u32[]{:S(2)}, u32[]{:S(2)}) collective-permute-start(bf16[64,256]{1,0:T(8,128)(2,1)S(1)} %fusion.47), channel_id=1, source_target_pairs={{0,128},{4,132},{8,136},{12,140},{16,144},{20,148},{24,152},{28,15... | collective-permute-start | bytes 98312 | tf_op jit(solution)/shard_map/ppermute | solution.py:11
  173.2 13.3 %collective-permute-start.8 = (bf16[64,256]{1,0:T(8,128)(2,1)S(1)}, bf16[64,256]{1,0:T(8,128)(2,1)S(1)}, u32[]{:S(2)}, u32[]{:S(2)}) collective-permute-start(bf16[64,256]{1,0:T(8,128)(2,1)S(1)} %fusion.48), channel_id=1, source_target_pairs={{0,384},{4,388},{8,392},{12,396},{16,400},{20,404},{24,408},{28,41... | collective-permute-start | bytes 98312 | tf_op jit(solution)/shard_map/ppermute | solution.py:11
  186.5 9.7 %collective-permute-start.7 = (bf16[64,256]{1,0:T(8,128)(2,1)S(1)}, bf16[64,256]{1,0:T(8,128)(2,1)S(1)}, u32[]{:S(2)}, u32[]{:S(2)}) collective-permute-start(bf16[64,256]{1,0:T(8,128)(2,1)S(1)} %fusion.48), channel_id=1, source_target_pairs={{384,0},{388,4},{392,8},{396,12},{400,16},{404,20},{408,24},{412,2... | collective-permute-start | bytes 98312 | tf_op jit(solution)/shard_map/ppermute | solution.py:11
  196.2 2.9 %collective-permute-start.6 = (bf16[64,256]{1,0:T(8,128)(2,1)S(1)}, bf16[64,256]{1,0:T(8,128)(2,1)S(1)}, u32[]{:S(2)}, u32[]{:S(2)}) collective-permute-start(bf16[64,256]{1,0:T(8,128)(2,1)S(1)} %fusion.48), channel_id=1, source_target_pairs={{0,256},{4,260},{8,264},{12,268},{16,272},{20,276},{24,280},{28,28... | collective-permute-start | bytes 98312 | tf_op jit(solution)/shard_map/ppermute | solution.py:11
  199.0 14.5 %collective-permute-start.5 = (bf16[64,256]{1,0:T(8,128)(2,1)S(1)}, bf16[64,256]{1,0:T(8,128)(2,1)S(1)}, u32[]{:S(2)}, u32[]{:S(2)}) collective-permute-start(bf16[64,256]{1,0:T(8,128)(2,1)S(1)} %fusion.48), channel_id=1, source_target_pairs={{256,0},{260,4},{264,8},{268,12},{272,16},{276,20},{280,24},{284,2... | collective-permute-start | bytes 98312 | tf_op jit(solution)/shard_map/ppermute | solution.py:11
  213.5 1.3 copy-start.5
  213.5 9.8 %collective-permute-start.9 = (bf16[64,256]{1,0:T(8,128)(2,1)S(1)}, bf16[64,256]{1,0:T(8,128)(2,1)}, u32[]{:S(2)}, u32[]{:S(2)}) collective-permute-start(bf16[64,256]{1,0:T(8,128)(2,1)S(1)} %fusion.47), channel_id=1, source_target_pairs={{128,0},{132,4},{136,8},{140,12},{144,16},{148,20},{152,24},{156,2... | collective-permute-start | bytes 98312 | tf_op jit(solution)/shard_map/ppermute | solution.py:11
  242.7 2.7 %copy-start.3 = (bf16[1,4,512,512]{3,2,1,0:T(8,128)(2,1)S(1)}, bf16[1,4,512,512]{3,2,1,0:T(8,128)(2,1)}, u32[]{:S(2)}) copy-start(bf16[1,4,512,512]{3,2,1,0:T(8,128)(2,1)} %param.18) | copy-start | bytes 6291460
Sparse Core Ops, SparseCore 0:
  46.1 48.9 all-gather.1
